TPU v7x, 1024 devices: a whole 4x4x32 slice. The times are simulated.
1024 devices in a mesh: dp: 16 (over y, x), seq: 64 (over z, core).
Axes of the slice: x: 4, y: 4, z: 32, core: 2. Of those that a mesh axis runs over, the one named last changes fastest.
Arguments:
- qkvu: bfloat16 [131072, 4096], P(('dp', 'seq')), may hold values from -6 to 6
- w_out: bfloat16 [1024, 1024], replicated, may hold values from -0.1875 to 0.1875
- head_coef: bfloat16 [131072, 256], P(('dp', 'seq')), may hold values from -0.375 to 0.375
- item_table: bfloat16 [32768, 1024], P('seq'), may hold values from -6 to 6
- neg_ids: int32 [256], P('seq'), may hold values from 0 to 511
- send_order: int32 [1024, 128], P(('dp', 'seq')), may hold values from 0 to 127, each once within a row
- recv_order: int32 [1024, 128], P(('dp', 'seq')), may hold values from 0 to 127, each once within a row
- tile_len: int32 [16, 64], P('dp'), may hold values from 1 to 128, 2730 in all within a row
Outputs:
- layer_out: bfloat16 [131072, 1024], P(('dp', 'seq'))
- d_qkvu: bfloat16 [131072, 4096], P(('dp', 'seq'))
- d_w_out: float32 [1024, 1024], P('seq', 'dp')
Inputs may be any that keep to these rules, and one draw needn't show every extreme that they name: Each row of send_order and of recv_order names every number once. `recv_order`: each row names every number once. `tile_len`: in each data group the lengths sum to 2730.
All inputs are finite; a program needn't handle non-finite values.
Results may differ from a plain program's by a relative error of at most 0.014.
Values may be sent and summed in bfloat16 or wider, within the bound.
A program may use at most 32 MiB of HBM per device.

v0:
```python
import math

import jax
import jax.numpy as jnp
from jax import lax
from jax.sharding import PartitionSpec as P

HEADS = 8
SPAN = 3


eps = 1e-05


def shifted(block, axis, distance):
    devices = range(lax.axis_size(axis))
    route = [(i - distance, i) for i in devices if i - distance in devices]
    return lax.ppermute(block, axis, route)


def silu_grad(values):
    sigmoid_val = jax.nn.sigmoid(values)
    return sigmoid_val * (1.0 + values * (1.0 - sigmoid_val))


def pair_mask(count, len_p, len_q, allowed, causal):
    positions = jnp.arange(count, dtype=jnp.int32)
    live = (positions[:, None] < len_p) & (positions[None, :] < len_q) & allowed
    if causal:
        live = live & (positions[None, :] <= positions[:, None])
    return jnp.where(live, 1.0, 0.0).astype(jnp.float32)


def head_major(flat, count, head_dim):
    return flat.reshape(count, HEADS, head_dim).transpose(1, 0, 2)


def row_major(heads_first, count, width):
    return heads_first.transpose(1, 0, 2).reshape(count, width)


def on_device(qkvu, w_out, head_coef, item_table, neg_ids, send_order, recv_order, tile_len):
    row_count = qkvu.shape[0]
    model_width = w_out.shape[0]
    head_dim = model_width // HEADS
    score_scale = 1.0 / math.sqrt(head_dim)
    send_list = send_order[0]
    recv_list = recv_order[0]
    own_index = lax.axis_index("seq")
    lengths_row = tile_len[0]
    own_len = jnp.take(lengths_row, own_index)
    outgoing = jnp.take(qkvu, send_list, axis=0)
    received = lax.all_to_all(outgoing, "seq", split_axis=0, concat_axis=0, tiled=True)
    balanced = jnp.take(received, recv_list, axis=0)
    neg_all = lax.all_gather(jnp.take(item_table, neg_ids, axis=0), "seq", axis=0, tiled=True)
    u_part = balanced[:, :model_width].astype(jnp.float32)
    value_heads = head_major(balanced[:, model_width : 2 * model_width], row_count, head_dim)
    query_heads = head_major(balanced[:, 2 * model_width : 3 * model_width], row_count, head_dim)
    key_heads = head_major(balanced[:, 3 * model_width :], row_count, head_dim)
    lagged = []
    carried = (value_heads, key_heads)
    for lag in range(1, SPAN):
        carried = shifted((carried[0], carried[1]), "seq", 1)
        lagged.append(carried)
    value_list = [value_heads]
    key_list = [key_heads]
    mask_list = [pair_mask(row_count, own_len, own_len, True, True)]
    for lag in range(1, SPAN):
        earlier_len = jnp.take(lengths_row, jnp.maximum(own_index - lag, 0))
        value_list.append(lagged[lag - 1][0])
        key_list.append(lagged[lag - 1][1])
        mask_list.append(pair_mask(row_count, own_len, earlier_len, own_index >= lag, False))
    values_all = jnp.concatenate(value_list, axis=1)
    keys_all = jnp.concatenate(key_list, axis=1)
    mask_all = jnp.concatenate(mask_list, axis=1)
    scores = (
        jnp.einsum("hpd,hqd->hpq", query_heads, keys_all, preferred_element_type=jnp.float32)
        * score_scale
    )
    weights = (jax.nn.silu(scores) * mask_all[None] / row_count).astype(jnp.bfloat16)
    attended_heads = jnp.einsum(
        "hpq,hqd->hpd", weights, values_all, preferred_element_type=jnp.float32
    )
    attended = row_major(attended_heads, row_count, model_width)
    row_mean = jnp.mean(attended, axis=1, keepdims=True)
    centered = attended - row_mean
    variance = jnp.mean(centered * centered, axis=1, keepdims=True)
    inv_std = lax.rsqrt(variance + eps)
    normed = centered * inv_std
    mixed_rows = (normed * u_part).astype(jnp.bfloat16)
    layer_out = jnp.dot(mixed_rows, w_out, preferred_element_type=jnp.float32).astype(jnp.bfloat16)
    positions = jnp.arange(row_count, dtype=jnp.int32)
    live_col = jnp.where(positions < own_len, 1.0, 0.0).astype(jnp.float32)[:, None]
    coef_live = (head_coef * live_col).astype(jnp.bfloat16)
    head_grad = jnp.dot(coef_live, neg_all, preferred_element_type=jnp.float32).astype(jnp.bfloat16)
    d_mixed = lax.dot_general(
        head_grad, w_out, (((1,), (1,)), ((), ())), preferred_element_type=jnp.float32
    )
    d_u_part = d_mixed * normed
    d_normed = d_mixed * u_part
    d_att = (
        d_normed
        - jnp.mean(d_normed, axis=1, keepdims=True)
        - normed * jnp.mean(d_normed * normed, axis=1, keepdims=True)
    ) * inv_std
    d_att_heads = head_major(d_att.astype(jnp.bfloat16), row_count, head_dim)
    d_weights = jnp.einsum(
        "hpd,hqd->hpq", d_att_heads, values_all, preferred_element_type=jnp.float32
    )
    d_scores = (d_weights * mask_all[None] / row_count * silu_grad(scores) * score_scale).astype(
        jnp.bfloat16
    )
    d_query = jnp.einsum("hpq,hqd->hpd", d_scores, keys_all, preferred_element_type=jnp.float32)
    part_keys = jnp.einsum(
        "hpq,hpd->hqd", d_scores, query_heads, preferred_element_type=jnp.float32
    )
    part_values = jnp.einsum(
        "hpq,hpd->hqd", weights, d_att_heads, preferred_element_type=jnp.float32
    )
    key_grad = part_keys[:, :row_count]
    value_grad = part_values[:, :row_count]
    for lag in range(1, SPAN):
        block_keys = part_keys[:, lag * row_count : (lag + 1) * row_count].astype(jnp.bfloat16)
        block_values = part_values[:, lag * row_count : (lag + 1) * row_count].astype(jnp.bfloat16)
        back_values, back_keys = shifted((block_values, block_keys), "seq", -lag)
        key_grad = key_grad + back_keys.astype(jnp.float32)
        value_grad = value_grad + back_values.astype(jnp.float32)
    tile_grads = jnp.concatenate(
        [
            d_u_part,
            row_major(value_grad, row_count, model_width),
            row_major(d_query, row_count, model_width),
            row_major(key_grad, row_count, model_width),
        ],
        axis=1,
    ).astype(jnp.bfloat16)
    slot_grads = jnp.zeros_like(tile_grads).at[recv_list].set(tile_grads)
    returned = lax.all_to_all(slot_grads, "seq", split_axis=0, concat_axis=0, tiled=True)
    d_home = jnp.zeros_like(returned).at[send_list].set(returned)
    coef_sums = lax.psum_scatter(
        lax.dot_general(
            mixed_rows, coef_live, (((0,), (0,)), ((), ())), preferred_element_type=jnp.float32
        ),
        "seq",
        scatter_dimension=0,
        tiled=True,
    )
    row_grad = jnp.dot(coef_sums, neg_all.astype(jnp.float32), precision=lax.Precision.HIGHEST)
    d_w_out = lax.psum_scatter(
        row_grad.astype(jnp.bfloat16), "dp", scatter_dimension=1, tiled=True
    ).astype(jnp.float32)
    return (layer_out, d_home, d_w_out)


def solution(mesh):
    placed = (
        P(("dp", "seq"), None),
        P(),
        P(("dp", "seq"), None),
        P("seq", None),
        P("seq"),
        P(("dp", "seq"), None),
        P(("dp", "seq"), None),
        P("dp", None),
    )
    return jax.shard_map(
        on_device,
        mesh=mesh,
        in_specs=placed,
        out_specs=(P(("dp", "seq"), None), P(("dp", "seq"), None), P("seq", "dp")),
        check_vma=False,
    )
```

profile of v0, /device:TPU:2, one launch (start us, length us, event | category | flops | bytes accessed | tf_op | source)
XLA Modules:
  0.0 651.6 jit_solution(16501900497779165659)
XLA Ops:
  8.7 3.6 gather_fusion.1
  13.4 2.5 all_to_all.16
  15.9 29.8 %all-to-all-start = ((bf16[64,2,4096]{2,1,0:T(2,128)(2,1)}), bf16[64,2,4096]{2,1,0:T(2,128)(2,1)}, u32[]{:S(2)}, u32[]{:S(2)}) async-start(bf16[64,2,4096]{2,1,0:T(2,128)(2,1)} %all_to_all.16), calls=%async_computation | async-start | bytes 2097152 | tf_op jit(solution)/shard_map/all_to_all | solution.py:53
  48.3 1.9 gather_fusion
  51.1 102.9 %all-to-all-done = bf16[64,2,4096]{2,1,0:T(2,128)(2,1)} async-done(((bf16[64,2,4096]{2,1,0:T(2,128)(2,1)}), bf16[64,2,4096]{2,1,0:T(2,128)(2,1)}, u32[]{:S(2)}, u32[]{:S(2)}) %all-to-all-start) | async-done | bytes 1048608 | tf_op jit(solution)/shard_map/all_to_all | solution.py:53
  155.4 2.2 gather_fusion.2
  161.8 2.1 collective-permute-start
  164.0 1.5 pad_maximum_fusion.6
  165.5 59.6 %all-gather = bf16[64,4,1024]{2,1,0:T(4,128)(2,1)} all-gather(bf16[1,4,1024]{2,1,0:T(4,128)(2,1)S(1)} %select_bitcast_fusion), channel_id=1, replica_groups=mesh['dp'=16,'seq'=64] {'seq'}, dimensions={0}, use_global_device_ids=true | all-gather | bytes 532480 | tf_op jit(solution)/shard_map/all_gather | solution.py:55
  225.1 1.8 copy.39
  226.9 3.0 collective-permute-start.2
  229.9 2.7 collective-permute-start.1
  232.6 2.0 reshape.297
  236.6 1.5 collective-permute-start.3
  238.1 3.1 multiply_convert_fusion.1
  242.1 2.3 fusion.37
  244.5 2.0 copy.40
  247.7 3.0 fusion.24
  250.8 2.3 multiply_convert_fusion.2
  253.1 1.9 multiply_convert_fusion
  255.1 1.5 fusion.38
  260.2 1.6 fusion.39
  264.0 1.5 collective-permute-start.4
  265.5 1.5 convolution_convert_fusion
  269.9 6.4 collective-permute-done.5
  278.4 3.0 scatter_custom_fusion
  281.4 1.5 all_to_all.19
  282.9 12.7 %all-to-all-start.1 = ((bf16[64,2,4096]{2,1,0:T(2,128)(2,1)}), bf16[64,2,4096]{2,1,0:T(2,128)(2,1)}, u32[]{:S(2)}, u32[]{:S(2)}) async-start(bf16[64,2,4096]{2,1,0:T(2,128)(2,1)} %all_to_all.19), calls=%async_computation.1 | async-start | bytes 2097152 | tf_op jit(solution)/shard_map/all_to_all | solution.py:138
  297.1 232.0 %reduce-scatter.5.cloned.1.call-done = f32[16,256]{1,0:T(8,128)} async-done(((f32[1024,256]{1,0:T(8,128)}), f32[16,256]{1,0:T(8,128)}) %reduce-scatter.5.cloned.1.call-update) | async-done | bytes 16400 | tf_op jit(solution)/shard_map/reduce_scatter | solution.py:140
  532.2 106.7 %reduce-scatter.7.cloned.1.call-done = bf16[64,16]{1,0:T(8,128)(2,1)} async-done(((bf16[1024,16]{1,0:T(8,128)(2,1)}), bf16[64,16]{1,0:T(8,128)(2,1)}) %reduce-scatter.7.cloned.1.call-update) | async-done | bytes 2064
  640.3 1.5 reshape.289
  641.8 3.0 scatter_custom_fusion.1
  (91 shorter events, 30.5 us)
Async XLA Ops:
  7.2 240.6 %copy-start = (bf16[1024,1024]{1,0:T(8,128)(2,1)S(1)}, bf16[1024,1024]{1,0:T(8,128)(2,1)}, u32[]{:S(2)}) copy-start(bf16[1024,1024]{1,0:T(8,128)(2,1)} %param.11) | copy-start | bytes 6291460
  15.9 29.8 %copy-start.9 = (s32[1,64]{1,0:T(1,128)S(1)}, s32[1,64]{1,0:T(1,128)}, u32[]{:S(2)}) copy-start(s32[1,64]{1,0:T(1,128)} %param.17) | copy-start | bytes 772
  15.9 32.3 %copy-start.12 = (s32[4]{0:T(128)S(1)}, s32[4]{0:T(128)}, u32[]{:S(2)}) copy-start(s32[4]{0:T(128)} %param.14) | copy-start | bytes 52
  15.9 34.3 %copy-start.13 = (s32[1,128]{1,0:T(1,128)S(1)}, s32[1,128]{1,0:T(1,128)}, u32[]{:S(2)}) copy-start(s32[1,128]{1,0:T(1,128)} %param.16) | copy-start | bytes 1540
  15.9 138.0 %all-to-all-start = ((bf16[64,2,4096]{2,1,0:T(2,128)(2,1)}), bf16[64,2,4096]{2,1,0:T(2,128)(2,1)}, u32[]{:S(2)}, u32[]{:S(2)}) async-start(bf16[64,2,4096]{2,1,0:T(2,128)(2,1)} %all_to_all.16), calls=%async_computation | async-start | bytes 2097152 | tf_op jit(solution)/shard_map/all_to_all | solution.py:53
  161.8 68.1 %collective-permute-start = (bf16[8,128,128]{2,1,0:T(8,128)(2,1)}, bf16[8,128,128]{2,1,0:T(8,128)(2,1)}, u32[]{:S(2)}, u32[]{:S(2)}) collective-permute-start(bf16[8,128,128]{2,1,0:T(8,128)(2,1)} %bitcast.94), channel_id=1, source_target_pairs={{0,1},{1,2},{2,3},{3,4},{4,5},{5,6},{6,7},{7,8},{8,9},{9,10},{10,1... | collective-permute-start | bytes 786440 | tf_op jit(solution)/shard_map/ppermute | solution.py:18
  226.9 9.6 %collective-permute-start.2 = (bf16[8,128,128]{1,2,0:T(8,128)(2,1)}, bf16[8,128,128]{1,2,0:T(8,128)(2,1)}, u32[]{:S(2)}, u32[]{:S(2)}) collective-permute-start(bf16[8,128,128]{1,2,0:T(8,128)(2,1)} %bitcast.16), channel_id=1, source_target_pairs={{0,1},{1,2},{2,3},{3,4},{4,5},{5,6},{6,7},{7,8},{8,9},{9,10},{10,1... | collective-permute-start | bytes 786440 | tf_op jit(solution)/shard_map/ppermute | solution.py:18
  229.9 8.2 %collective-permute-start.1 = (bf16[8,128,128]{2,1,0:T(8,128)(2,1)}, bf16[8,128,128]{2,1,0:T(8,128)(2,1)}, u32[]{:S(2)}, u32[]{:S(2)}) collective-permute-start(bf16[8,128,128]{2,1,0:T(8,128)(2,1)} %collective-permute-done), channel_id=1, source_target_pairs={{0,1},{1,2},{2,3},{3,4},{4,5},{5,6},{6,7},{7,8},{8,9},{9,10},{10,1... | collective-permute-start | bytes 786440 | tf_op jit(solution)/shard_map/ppermute | solution.py:18
  235.7 5.6 copy-start.2
  236.6 4.7 collective-permute-start.3
  241.3 0.9 copy-start.4
  241.3 3.2 copy-start.10
  242.1 5.6 copy-start.6
  250.7 2.4 copy-start.8
  250.7 2.4 copy-start.11
  250.7 2.4 copy-start.15
  253.1 1.9 copy-start.3
  256.6 3.6 copy-start.5
  257.6 10.3 %collective-permute-start.7 = (bf16[8,128,128]{1,2,0:T(8,128)(2,1)}, bf16[8,128,128]{1,2,0:T(8,128)(2,1)S(1)}, u32[]{:S(2)}, u32[]{:S(2)}) collective-permute-start(bf16[8,128,128]{1,2,0:T(8,128)(2,1)} %get-tuple-element.48), channel_id=1, source_target_pairs={{2,0},{3,1},{4,2},{5,3},{6,4},{7,5},{8,6},{9,7},{10,8},{11,9},{12,... | collective-permute-start | bytes 786440 | tf_op jit(solution)/shard_map/ppermute | solution.py:18
  258.8 9.0 %collective-permute-start.6 = (bf16[8,128,128]{1,2,0:T(8,128)(2,1)}, bf16[8,128,128]{1,2,0:T(8,128)(2,1)S(1)}, u32[]{:S(2)}, u32[]{:S(2)}) collective-permute-start(bf16[8,128,128]{1,2,0:T(8,128)(2,1)} %get-tuple-element.47), channel_id=1, source_target_pairs={{1,0},{2,1},{3,2},{4,3},{5,4},{6,5},{7,6},{8,7},{9,8},{10,9},{11,1... | collective-permute-start | bytes 786440 | tf_op jit(solution)/shard_map/ppermute | solution.py:18
  260.2 5.3 copy-start.7
  262.7 13.6 %collective-permute-start.5 = (bf16[8,128,128]{1,2,0:T(8,128)(2,1)}, bf16[8,128,128]{1,2,0:T(8,128)(2,1)S(1)}, u32[]{:S(2)}, u32[]{:S(2)}) collective-permute-start(bf16[8,128,128]{1,2,0:T(8,128)(2,1)} %get-tuple-element.46), channel_id=1, source_target_pairs={{2,0},{3,1},{4,2},{5,3},{6,4},{7,5},{8,6},{9,7},{10,8},{11,9},{12,... | collective-permute-start | bytes 786440 | tf_op jit(solution)/shard_map/ppermute | solution.py:18
  264.0 12.3 %collective-permute-start.4 = (bf16[8,128,128]{1,2,0:T(8,128)(2,1)}, bf16[8,128,128]{1,2,0:T(8,128)(2,1)}, u32[]{:S(2)}, u32[]{:S(2)}) collective-permute-start(bf16[8,128,128]{1,2,0:T(8,128)(2,1)} %get-tuple-element.45), channel_id=1, source_target_pairs={{1,0},{2,1},{3,2},{4,3},{5,4},{6,5},{7,6},{8,7},{9,8},{10,9},{11,1... | collective-permute-start | bytes 786440 | tf_op jit(solution)/shard_map/ppermute | solution.py:18
  282.9 357.4 %all-to-all-start.1 = ((bf16[64,2,4096]{2,1,0:T(2,128)(2,1)}), bf16[64,2,4096]{2,1,0:T(2,128)(2,1)}, u32[]{:S(2)}, u32[]{:S(2)}) async-start(bf16[64,2,4096]{2,1,0:T(2,128)(2,1)} %all_to_all.19), calls=%async_computation.1 | async-start | bytes 2097152 | tf_op jit(solution)/shard_map/all_to_all | solution.py:138
  295.6 1.5 copy-start.14
  295.7 233.5 %copy-start.1 = (bf16[256,1024]{1,0:T(8,128)(2,1)S(1)}, bf16[256,1024]{1,0:T(8,128)(2,1)}, u32[]{:S(2)}) copy-start(bf16[256,1024]{1,0:T(8,128)(2,1)} %reshape.297) | copy-start | bytes 1572868
  295.7 233.5 %reduce-scatter.5.cloned.1.call-start = ((), (), s32[]{:S(2)}) async-start(), calls=%async_computation.4 | async-start | bytes 1064960 | tf_op jit(solution)/shard_map/reduce_scatter | solution.py:140
  297.1 341.8 %reduce-scatter.7.cloned.1.call-start = ((), (), s32[]{:S(2)}) async-start(), calls=%async_computation.5 | async-start | bytes 278528
Sparse Core Ops, SparseCore 0:
  299.8 229.2 reduce-scatter.4
  534.4 104.4 reduce-scatter.6
where the time goes:
time: 653 us; the launch traced here: 652 us
  waiting for transfers between devices  448 us (69%)
  blocking collectives  59.6 us (9%)
  starting transfers between devices  57.2 us (9%)
  local copies, waits for them, and re-layouts  36 us (6%)
  matrix products  18.5 us (3%)
  between operations  16.3 us (2%)
  other arithmetic  15.9 us (2%)
    reduce_scatter x1, waiting for transfers between devices, on_device(): lax.psum_scatter(lax.dot_general(mixed_rows, coef_live, (((0,), (0,)), ((...  232 us
    unnamed x3, waiting for transfers between devices  107 us
    all_to_all x1, waiting for transfers between devices, on_device(): lax.all_to_all(outgoing, 'seq', split_axis=0, concat_axis=0, tiled=True)  103 us
    all_gather x1, blocking collectives, on_device(): lax.all_gather(jnp.take(item_table, neg_ids, axis=0), 'seq', axis=0, tile...  59.6 us
    all_to_all x1, starting transfers between devices, on_device(): lax.all_to_all(outgoing, 'seq', split_axis=0, concat_axis=0, tiled=True)  29.8 us
    ppermute x8, starting transfers between devices, shifted(): return lax.ppermute(block, axis, route)  14.7 us
  transfers between devices with their start and end apart: 12, of which 4 were waited for; matrix products, arithmetic and copies ran while one was open for 4% of the time, Pallas kernels for 0%

commit v1 on v0

v1 whole, which is shorter than its diff:
```python
import functools
import math

import jax
import jax.numpy as jnp
from jax import lax
from jax.experimental import pallas as pl
from jax.experimental.pallas import tpu as pltpu
from jax.sharding import PartitionSpec as P

HEADS = 8
SPAN = 3
CH = 256
eps = 1e-05
BF = jnp.bfloat16
F32 = jnp.float32
MESH = pl.DeviceIdType.MESH


def iota(shape, dim):
    return lax.broadcasted_iota(jnp.int32, shape, dim)


def mm(a, b):
    return jnp.dot(a, b, preferred_element_type=F32)


def mm_nt(a, b):
    return lax.dot_general(a, b, (((1,), (1,)), ((), ())), preferred_element_type=F32)


def mm_tn(a, b):
    return lax.dot_general(a, b, (((0,), (0,)), ((), ())), preferred_element_type=F32)


def kernel(
    n_dp, n_seq,
    ids_ref, len_ref, qkvu_ref, w_ref, coef_ref, table_ref, send_ref, recv_ref,
    out_ref, home_ref, dw_ref,
    put_ref, get_ref, put_back_ref, get_back_ref, stack_ref,
    xkv, xuq, rkv, ruq, gkv, guq, hkv, huq,
    kv_ref, uq_ref, own_ref, duq_ref, part_ref, back_ref,
    wgt_ref, fac_ref, mask_ref, att_ref, datt_ref, mixed_ref, live_ref, dmix_ref,
    negs_ref, neg_ref, sum_x, sum_r, sum_z, sum_zr, sum_f,
    a2a_send, a2a_recv, neg_send, neg_zrecv, neg_xsend, neg_xrecv,
    halo_send, halo_recv, back_send, back_recv,
    sx_send, sx_recv, sz_send, sz_recv, sf_send, sf_recv,
):
    g = lax.axis_index("dp")
    t = lax.axis_index("seq")
    rows, width = att_ref.shape
    slots = 8 * rows
    head = width // HEADS
    scale = 1.0 / math.sqrt(head)
    per_ring = n_seq // n_dp
    d_rows = width // n_seq
    rb = slots // n_seq
    my_turn = lax.rem(t, n_dp) == g

    def rcopy(src, dst, ssem, rsem, **where):
        return pltpu.make_async_remote_copy(
            src_ref=src, dst_ref=dst, send_sem=ssem, recv_sem=rsem,
            device_id=where, device_id_type=MESH,
        )

    def each_seq_peer(body):
        def step(i, c):
            body(lax.rem(t + i, n_seq))
            return c
        lax.fori_loop(1, n_seq, step, 0)

    def far_first(body):
        half = n_seq // 2

        def step(i, c):
            k = half - i
            body(lax.rem(t + k, n_seq))

            @pl.when(k < half)
            def _():
                body(lax.rem(t + n_seq - k, n_seq))
            return c
        lax.fori_loop(0, half, step, 0)

    def each_dp_peer(body):
        def step(i, c):
            body(lax.rem(g + i, n_dp))
            return c
        lax.fori_loop(1, n_dp, step, 0)

    barrier = pltpu.get_barrier_semaphore()
    each_seq_peer(lambda s: pl.semaphore_signal(barrier, inc=1, device_id={"seq": s}, device_id_type=MESH))
    each_dp_peer(lambda d: pl.semaphore_signal(barrier, inc=1, device_id={"dp": d}, device_id_type=MESH))

    send_f = send_ref[...].astype(F32)
    recv_f = recv_ref[...].astype(F32)
    one = lambda m: jnp.where(m, 1.0, 0.0).astype(BF)

    def build_put(b, c):
        i0 = iota((rows, rows), 0)
        l0 = iota((rows, rows), 1)
        slot = b * (rows // 8) + lax.shift_right_logical(i0, 3)
        idx = jnp.sum(jnp.where(l0 == slot, send_f, 0.0), axis=1, keepdims=True)
        i = iota((rows, slots), 0)
        l = iota((rows, slots), 1)
        m = (idx == (l & (rows - 1)).astype(F32)) & ((i & 7) == lax.shift_right_logical(l, 7))
        put_ref[pl.ds(pl.multiple_of(b * rows, rows), rows), :] = one(m)
        return c

    lax.fori_loop(0, 8, build_put, 0)

    r = iota((16, 512), 0)
    l = iota((16, 512), 1)
    j = r & 3
    pick = jnp.where(j == 0, ids_ref[0], jnp.where(j == 1, ids_ref[1], jnp.where(j == 2, ids_ref[2], ids_ref[3])))
    hit = l == pick
    block = jnp.zeros((16, CH), F32)
    for q in range(4):
        block = block + mm(one(hit & (lax.shift_right_logical(r, 2) == q)), table_ref[:, q * CH:(q + 1) * CH])

    @pl.when(my_turn)
    def _():
        negs_ref[g * per_ring + lax.div(t, n_dp)] = block.astype(BF)

    def stack(ref, starts):
        for n, c in enumerate(starts):
            stack_ref[n * rows:(n + 1) * rows, :] = ref[:, c:c + CH]

    kv_cols = [width + n * CH for n in range(4)] + [3 * width + n * CH for n in range(4)]
    uq_cols = [n * CH for n in range(4)] + [2 * width + n * CH for n in range(4)]
    half_cols = [n * CH for n in range(8)]

    def to_blocks(mat, dst):
        nb = 256 // rb
        for b in range(slots // 256):
            y = mm(mat[b * 256:(b + 1) * 256, :], stack_ref[...]).astype(BF)
            dst[b * nb:(b + 1) * nb] = y.reshape(nb, rb, CH)

    def from_blocks(mat, src, write):
        v = src[...].reshape(slots, CH)
        per = 256 // rows
        for b in range(slots // 256):
            y = mm(mat[b * 256:(b + 1) * 256, :], v).astype(BF)
            for n in range(per):
                write(b * per + n, y[n * rows:(n + 1) * rows])

    def a2a(n, src, dst):
        dst[t] = src[t]
        far_first(lambda s: rcopy(src.at[s], dst.at[t], a2a_send.at[n], a2a_recv.at[n], seq=s).start())

    def take(buf, sem, count):
        v = buf.at[pl.ds(0, count)]
        pltpu.make_async_copy(v, v, sem).wait()

    stack(qkvu_ref, kv_cols)
    to_blocks(put_ref, xkv)

    pl.semaphore_wait(barrier, n_seq - 1 + n_dp - 1)

    @pl.when(my_turn)
    def _():
        mine = negs_ref.at[g * per_ring + lax.div(t, n_dp)]
        far_first(lambda s: rcopy(mine, mine, neg_send, neg_zrecv.at[lax.div(t, n_dp)], seq=s).start())

    a2a(0, xkv, rkv)
    stack(qkvu_ref, uq_cols)
    to_blocks(put_ref, xuq)
    a2a(1, xuq, ruq)

    i0 = iota((rows, rows), 0)
    l0 = iota((rows, rows), 1)
    send_col = jnp.sum(jnp.where(i0 == l0, send_f, 0.0), axis=1, keepdims=True)
    recv_col = jnp.sum(jnp.where(i0 == l0, recv_f, 0.0), axis=1, keepdims=True)

    def build_rows(j, c):
        l = iota((rows, slots), 1)
        i = iota((rows, slots), 0)
        slot = lax.shift_right_logical(l, 3)
        turn = (l & 7) == j
        at = pl.ds(pl.multiple_of(j * rows, rows), rows)
        get_ref[at, :] = one((recv_col == slot.astype(F32)) & turn)
        send_row = jnp.sum(jnp.where(i == slot, send_col, 0.0), axis=0, keepdims=True)
        get_back_ref[at, :] = one((send_row == i.astype(F32)) & turn)
        recv_row = jnp.concatenate([recv_f] * 8, axis=1)
        put_slot = j * (rows // 8) + lax.shift_right_logical(i, 3)
        put_back_ref[at, :] = one((recv_row == put_slot.astype(F32)) & ((i & 7) == lax.shift_right_logical(l, 7)))
        return c

    lax.fori_loop(0, 8, build_rows, 0)

    own_len = len_ref[0, t]
    len_1 = jnp.where(t >= 1, len_ref[0, lax.max(t - 1, 0)], 0)
    len_2 = jnp.where(t >= 2, len_ref[0, lax.max(t - 2, 0)], 0)
    alive = i0 < own_len
    for n, m in enumerate((alive & (l0 <= i0) & (l0 < own_len), alive & (l0 < len_1), alive & (l0 < len_2))):
        mask_ref[:, n * rows:(n + 1) * rows] = jnp.where(m, 1.0 / rows, 0.0)

    live_col = jnp.where(iota(coef_ref.shape, 0) < own_len, 1.0, 0.0)
    live_ref[...] = (coef_ref[...].astype(F32) * live_col).astype(BF)

    for k in range(per_ring):
        @pl.when(k * n_dp + g != t)
        def _():
            v = negs_ref.at[g * per_ring + k]
            pltpu.make_async_copy(v, v, neg_zrecv.at[k]).wait()
    shards = negs_ref.at[pl.ds(g * per_ring, per_ring)]
    each_dp_peer(lambda d: rcopy(shards, shards, neg_xsend, neg_xrecv, dp=d).start())
    take(negs_ref, neg_xrecv, (n_dp - 1) * per_ring)

    n_negs = 4 * n_seq
    flat = negs_ref[...].reshape(16 * n_seq, CH)
    n = iota((n_negs, 16 * n_seq), 0)
    l = iota((n_negs, 16 * n_seq), 1)
    shard = lax.shift_right_logical(n, 2)
    ring_bits = n_dp.bit_length() - 1
    place = ((shard & (n_dp - 1)) * per_ring + lax.shift_right_logical(shard, ring_bits)) * 16 + (n & 3)
    for q in range(4):
        neg_ref[:, q * CH:(q + 1) * CH] = mm(one(l == place + 4 * q), flat).astype(BF)

    head_grad = mm(live_ref[...], neg_ref[...]).astype(BF)
    for b in range(width // CH):
        dmix_ref[:, b * CH:(b + 1) * CH] = mm_nt(head_grad, w_ref[b * CH:(b + 1) * CH, :])

    take(rkv, a2a_recv.at[0], n_seq - 1)

    def write_kv(n, y):
        kv_ref[0, :, n * CH:(n + 1) * CH] = y
    from_blocks(get_ref, rkv, write_kv)
    for lag in range(1, SPAN):
        @pl.when(t + lag < n_seq)
        def _():
            rcopy(kv_ref.at[0], kv_ref.at[lag], halo_send.at[lag - 1], halo_recv.at[lag - 1], seq=lax.rem(t + lag, n_seq)).start()

        @pl.when(t < lag)
        def _():
            kv_ref[lag] = jnp.zeros(kv_ref.shape[1:], BF)

    take(ruq, a2a_recv.at[1], n_seq - 1)

    def write_uq(n, y):
        uq_ref[:, n * CH:(n + 1) * CH] = y
    from_blocks(get_ref, ruq, write_uq)
    for lag in range(1, SPAN):
        @pl.when(t >= lag)
        def _():
            pltpu.make_async_copy(kv_ref.at[lag], kv_ref.at[lag], halo_recv.at[lag - 1]).wait()

    def lanes(h, base=0):
        return pl.ds(pl.multiple_of(base + h * head, head), head)

    def forward(h, c):
        q = uq_ref[:, lanes(h, width)]
        k3 = kv_ref[:, :, lanes(h, width)].reshape(SPAN * rows, head)
        v3 = kv_ref[:, :, lanes(h)].reshape(SPAN * rows, head)
        s = mm_nt(q, k3) * scale
        sig = 0.5 + 0.5 * jnp.tanh(0.5 * s)
        m = mask_ref[...]
        w = (s * sig * m).astype(BF)
        wgt_ref[h] = w
        fac_ref[h] = m * scale * (sig * (1.0 + s * (1.0 - sig)))
        att_ref[:, lanes(h)] = mm(w, v3)
        return c

    lax.fori_loop(0, HEADS, forward, 0)

    step = 32
    for b in range(rows // step):
        at = slice(b * step, (b + 1) * step)
        a = att_ref[at, :]
        cen = a - jnp.mean(a, axis=1, keepdims=True)
        inv = lax.rsqrt(jnp.mean(cen * cen, axis=1, keepdims=True) + eps)
        normed = cen * inv
        u = uq_ref[at, :width].astype(F32)
        mixed_ref[at, :] = (normed * u).astype(BF)
        dm = dmix_ref[at, :]
        duq_ref[at, :width] = (dm * normed).astype(BF)
        dn = dm * u
        da = (dn - jnp.mean(dn, axis=1, keepdims=True) - normed * jnp.mean(dn * normed, axis=1, keepdims=True)) * inv
        datt_ref[at, :] = da.astype(BF)

    def backward(h, c):
        q = uq_ref[:, lanes(h, width)]
        k3 = kv_ref[:, :, lanes(h, width)].reshape(SPAN * rows, head)
        v3 = kv_ref[:, :, lanes(h)].reshape(SPAN * rows, head)
        da = datt_ref[:, lanes(h)]
        ds = (mm_nt(da, v3) * fac_ref[h]).astype(BF)
        duq_ref[:, lanes(h, width)] = mm(ds, k3).astype(BF)
        kp = mm_tn(ds, q)
        vp = mm_tn(wgt_ref[h], da)
        own_ref[:, lanes(h, width)] = kp[:rows]
        own_ref[:, lanes(h)] = vp[:rows]
        for lag in range(1, SPAN):
            part_ref[lag - 1, :, lanes(h, width)] = kp[lag * rows:(lag + 1) * rows].astype(BF)
            part_ref[lag - 1, :, lanes(h)] = vp[lag * rows:(lag + 1) * rows].astype(BF)
        return c

    lax.fori_loop(0, HEADS, backward, 0)

    for lag in range(1, SPAN):
        @pl.when(t >= lag)
        def _():
            rcopy(part_ref.at[lag - 1], back_ref.at[lag - 1], back_send.at[lag - 1], back_recv.at[lag - 1], seq=lax.rem(t + n_seq - lag, n_seq)).start()

        @pl.when(t + lag >= n_seq)
        def _():
            back_ref[lag - 1] = jnp.zeros(back_ref.shape[1:], BF)

    stack(duq_ref, half_cols)
    to_blocks(put_back_ref, guq)
    a2a(2, guq, huq)

    per_block = rows // d_rows
    for b in range(width // rows):
        y = mm_tn(mixed_ref[:, b * rows:(b + 1) * rows], live_ref[...])
        for n in range(per_block):
            s = b * per_block + n
            sum_x[s % n_dp, s // n_dp] = y[n * d_rows:(n + 1) * d_rows]
    sum_r[g] = sum_x[g]
    each_dp_peer(lambda d: rcopy(sum_x.at[d], sum_r.at[g], sx_send, sx_recv, dp=d).start())

    for b in range(width // CH):
        out_ref[:, b * CH:(b + 1) * CH] = mm(mixed_ref[...], w_ref[:, b * CH:(b + 1) * CH]).astype(BF)

    take(sum_r, sx_recv, n_dp - 1)
    sum_z[...] = lax.fori_loop(1, n_dp, lambda i, acc: acc + sum_r[i], sum_r[0])
    for k in range(per_ring):
        s = k * n_dp + g

        @pl.when(s != t)
        def _():
            rcopy(sum_z.at[k], sum_zr.at[t], sz_send.at[k], sz_recv, seq=s).start()

        @pl.when(s == t)
        def _():
            sum_zr[t] = sum_z[k]

    for lag in range(1, SPAN):
        @pl.when(t + lag < n_seq)
        def _():
            pltpu.make_async_copy(back_ref.at[lag - 1], back_ref.at[lag - 1], back_recv.at[lag - 1]).wait()
    for n in range(8):
        c = slice(n * CH, (n + 1) * CH)
        y = own_ref[:, c] + back_ref[0, :, c].astype(F32) + back_ref[1, :, c].astype(F32)
        stack_ref[n * rows:(n + 1) * rows, :] = y.astype(BF)
    to_blocks(put_back_ref, gkv)
    a2a(3, gkv, hkv)

    @pl.when(my_turn)
    def _():
        take(sum_zr, sz_recv, n_seq - 1)
        sum_f[...] = lax.fori_loop(1, n_seq, lambda i, acc: acc + sum_zr[i], sum_zr[0])
        each_dp_peer(lambda d: rcopy(sum_f, sum_f, sf_send, sf_recv, dp=d).start())

    @pl.when(jnp.logical_not(my_turn))
    def _():
        pltpu.make_async_copy(sum_f, sum_f, sf_recv).wait()

    total = sum_f[...]
    top = total.astype(BF)
    low = (total - top.astype(F32)).astype(BF)
    cols = width // n_dp
    if cols >= 128:
        nb = neg_ref[:, pl.ds(pl.multiple_of(g * cols, cols), cols)]
        dw_ref[...] = mm(top, nb) + mm(low, nb)
    else:
        per = 128 // cols
        nb = neg_ref[:, pl.ds(pl.multiple_of(lax.div(g, per) * 128, 128), 128)]
        y = mm(top, nb) + mm(low, nb)
        z = y[:, :cols]
        for n in range(1, per):
            z = jnp.where(lax.rem(g, per) == n, y[:, n * cols:(n + 1) * cols], z)
        dw_ref[...] = z

    take(huq, a2a_recv.at[2], n_seq - 1)

    def home_uq(n, y):
        home_ref[:, uq_cols[n]:uq_cols[n] + CH] = y
    from_blocks(get_back_ref, huq, home_uq)
    take(hkv, a2a_recv.at[3], n_seq - 1)

    def home_kv(n, y):
        home_ref[:, kv_cols[n]:kv_cols[n] + CH] = y
    from_blocks(get_back_ref, hkv, home_kv)

    for n, buf in enumerate((xkv, xuq, guq, gkv)):
        take(buf, a2a_send.at[n], n_seq - 1)

    def sent(buf, sem):
        pltpu.make_async_copy(buf, buf, sem).wait()

    take(negs_ref, neg_xsend, (n_dp - 1) * per_ring)
    take(sum_x, sx_send, n_dp - 1)

    @pl.when(my_turn)
    def _():
        take(negs_ref, neg_send, n_seq - 1)
        take(sum_zr, sf_send, n_dp - 1)

    for k in range(per_ring):
        @pl.when(k * n_dp + g != t)
        def _():
            sent(sum_z.at[k], sz_send.at[k])
    for lag in range(1, SPAN):
        @pl.when(t + lag < n_seq)
        def _():
            sent(kv_ref.at[0], halo_send.at[lag - 1])

        @pl.when(t >= lag)
        def _():
            sent(part_ref.at[lag - 1], back_send.at[lag - 1])


def on_device(n_dp, n_seq, qkvu, w_out, head_coef, item_table, neg_ids, send_order, recv_order, tile_len):
    rows = qkvu.shape[0]
    width = w_out.shape[0]
    slots = 8 * rows
    rb = slots // n_seq
    per_ring = n_seq // n_dp
    d_rows = width // n_seq
    negs = head_coef.shape[1]
    vm = pl.BlockSpec(memory_space=pltpu.VMEM)
    sm = pl.BlockSpec(memory_space=pltpu.SMEM)
    dma = pltpu.SemaphoreType.DMA
    blocks = pltpu.VMEM((n_seq, rb, CH), BF)
    square = pltpu.VMEM((slots, slots), BF)
    return pl.pallas_call(
        functools.partial(kernel, n_dp, n_seq),
        out_shape=(
            jax.ShapeDtypeStruct((rows, width), BF),
            jax.ShapeDtypeStruct((rows, 4 * width), BF),
            jax.ShapeDtypeStruct((d_rows, width // n_dp), F32),
        ),
        in_specs=[sm, sm] + [vm] * 6,
        out_specs=(vm, vm, vm),
        scratch_shapes=[
            square, square, square, square, pltpu.VMEM((slots, CH), BF),
            blocks, blocks, blocks, blocks, blocks, blocks, blocks, blocks,
            pltpu.VMEM((SPAN, rows, 2 * width), BF),
            pltpu.VMEM((rows, 2 * width), BF),
            pltpu.VMEM((rows, 2 * width), F32),
            pltpu.VMEM((rows, 2 * width), BF),
            pltpu.VMEM((SPAN - 1, rows, 2 * width), BF),
            pltpu.VMEM((SPAN - 1, rows, 2 * width), BF),
            pltpu.VMEM((HEADS, rows, SPAN * rows), BF),
            pltpu.VMEM((HEADS, rows, SPAN * rows), F32),
            pltpu.VMEM((rows, SPAN * rows), F32),
            pltpu.VMEM((rows, width), F32),
            pltpu.VMEM((rows, width), BF),
            pltpu.VMEM((rows, width), BF),
            pltpu.VMEM((rows, negs), BF),
            pltpu.VMEM((rows, width), F32),
            pltpu.VMEM((n_seq, 16, CH), BF),
            pltpu.VMEM((negs, width), BF),
            pltpu.VMEM((n_dp, per_ring, d_rows, negs), F32),
            pltpu.VMEM((n_dp, per_ring, d_rows, negs), F32),
            pltpu.VMEM((per_ring, d_rows, negs), F32),
            pltpu.VMEM((n_seq, d_rows, negs), F32),
            pltpu.VMEM((d_rows, negs), F32),
            dma((4,)), dma((4,)), dma, dma((per_ring,)), dma, dma,
            dma((SPAN - 1,)), dma((SPAN - 1,)), dma((SPAN - 1,)), dma((SPAN - 1,)),
            dma, dma, dma((per_ring,)), dma, dma, dma,
        ],
        compiler_params=pltpu.CompilerParams(
            collective_id=0, has_side_effects=True, vmem_limit_bytes=60 * 2**20
        ),
    )(neg_ids, tile_len, qkvu, w_out, head_coef, item_table, send_order, recv_order)


def solution(mesh):
    placed = (
        P(("dp", "seq"), None),
        P(),
        P(("dp", "seq"), None),
        P("seq", None),
        P("seq"),
        P(("dp", "seq"), None),
        P(("dp", "seq"), None),
        P("dp", None),
    )
    return jax.shard_map(
        functools.partial(on_device, mesh.shape["dp"], mesh.shape["seq"]),
        mesh=mesh,
        in_specs=placed,
        out_specs=(P(("dp", "seq"), None), P(("dp", "seq"), None), P("seq", "dp")),
        check_vma=False,
    )
```

time: 653 us -> 276 us (0.42)
  the two profiles are of different devices: /device:TPU:2 before, /device:TPU:17 now
where the time goes in v1:
time: 276 us
  Pallas kernels  271 us (98%)
  local copies, waits for them, and re-layouts  4.56 us (2%)
    pallas_call x1, Pallas kernels, on_device(): pl.pallas_call(functools.partial(kernel, n_dp, n_seq), out_shape=(jax.Sha...  271 us

profile of v1, /device:TPU:17, one launch (start us, length us, event | category | flops | bytes accessed | tf_op | source)
XLA Modules:
  0.0 276.3 jit_solution(14734177325908121323)
XLA Ops:
  0.6 271.1 %shard_map.103 = (bf16[128,1024]{1,0:T(8,128)(2,1)}, bf16[128,4096]{1,0:T(8,128)(2,1)}, f32[16,64]{1,0:T(8,128)}) custom-call(s32[4]{0:T(128)} %ids_ref.1, s32[1,64]{1,0:T(1,128)} %len_ref.1, bf16[128,4096]{1,0:T(8,128)(2,1)} %qkvu_ref.1, bf16[1024,1024]{1,0:T(8,128)(2,1)} %w_ref.1, bf16[128,256]{1,0:T(8,128)(2,1)} %coef_ref.1, bf16[512,1024]{1,0:T(8,128)(2,1)} %table_ref.1, ...), custom_call_target="tpu_custom_call" | custom-call | tf_op jit(solution)/shard_map/pallas_call | solution.py:426
  271.7 0.0 copy-start
  271.7 1.7 copy.14
  273.4 2.3 copy.15
  275.7 0.0 copy-done
  275.7 0.6 copy.16
Async XLA Ops:
  271.7 4.0 %copy-start = (f32[16,64]{1,0:T(8,128)S(1)}, f32[16,64]{1,0:T(8,128)}, u32[]{:S(2)}) copy-start(f32[16,64]{1,0:T(8,128)} %get-tuple-element.8) | copy-start | bytes 12292

commit v2 on v1

--- a/solution.py
+++ b/solution.py
@@ -35,14 +35,16 @@
 
 def kernel(
     n_dp, n_seq,
-    ids_ref, len_ref, qkvu_ref, w_ref, coef_ref, table_ref, send_ref, recv_ref,
+    ids_ref, len_ref, qkvu_ref, coef_ref, send_ref, recv_ref, w_hbm, table_hbm,
     out_ref, home_ref, dw_ref,
-    put_ref, get_ref, put_back_ref, get_back_ref, stack_ref,
-    xkv, xuq, rkv, ruq, gkv, guq, hkv, huq,
-    kv_ref, uq_ref, own_ref, duq_ref, part_ref, back_ref,
-    wgt_ref, fac_ref, mask_ref, att_ref, datt_ref, mixed_ref, live_ref, dmix_ref,
+    w_ref, table_ref,
+    put_ref, get_ref, put_back_ref, get_back_ref, stack_ref, pair_ref, thin_ref,
+    xkv, rkv, gkv, hkv,
+    xq, xu, rq, ru, gq, gu, hq, hu,
+    kv_ref, q_ref, u_ref, own_ref, part_ref, back_ref,
+    wgt_ref, fac_ref, mask_ref, att_ref, inv_ref, datt_ref, mixed_ref, live_ref, dmix_ref,
     negs_ref, neg_ref, sum_x, sum_r, sum_z, sum_zr, sum_f,
-    a2a_send, a2a_recv, neg_send, neg_zrecv, neg_xsend, neg_xrecv,
+    load_sem, a2a_send, a2a_recv, neg_send, neg_zrecv, neg_xsend, neg_xrecv,
     halo_send, halo_recv, back_send, back_recv,
     sx_send, sx_recv, sz_send, sz_recv, sf_send, sf_recv,
 ):
@@ -92,6 +94,11 @@
     each_seq_peer(lambda s: pl.semaphore_signal(barrier, inc=1, device_id={"seq": s}, device_id_type=MESH))
     each_dp_peer(lambda d: pl.semaphore_signal(barrier, inc=1, device_id={"dp": d}, device_id_type=MESH))
 
+    load_table = pltpu.make_async_copy(table_hbm, table_ref, load_sem.at[0])
+    load_w = pltpu.make_async_copy(w_hbm, w_ref, load_sem.at[1])
+    load_table.start()
+    load_w.start()
+
     send_f = send_ref[...].astype(F32)
     recv_f = recv_ref[...].astype(F32)
     one = lambda m: jnp.where(m, 1.0, 0.0).astype(BF)
@@ -109,6 +116,46 @@
 
     lax.fori_loop(0, 8, build_put, 0)
 
+    def stack(starts):
+        for n, c in enumerate(starts):
+            stack_ref[n * rows:(n + 1) * rows, :] = qkvu_ref[:, c:c + CH]
+
+    kv_cols = [width + n * CH for n in range(4)] + [3 * width + n * CH for n in range(4)]
+
+    def to_blocks(mat, src, *dsts):
+        nb = 256 // rb
+        for b in range(slots // 256):
+            y = mm(mat[b * 256:(b + 1) * 256, :], src[...]).astype(BF)
+            w = y.shape[1] // len(dsts)
+            for n, dst in enumerate(dsts):
+                dst[b * nb:(b + 1) * nb] = y[:, n * w:(n + 1) * w].reshape(nb, rb, w)
+
+    def from_blocks(mat, v, write):
+        v = v.reshape(slots, v.shape[-1])
+        per = 256 // rows
+        for b in range(slots // 256):
+            y = mm(mat[b * 256:(b + 1) * 256, :], v).astype(BF)
+            for n in range(per):
+                write(b * per + n, y[n * rows:(n + 1) * rows])
+
+    def a2a(n, src, dst):
+        dst[t] = src[t]
+        far_first(lambda s: rcopy(src.at[s], dst.at[t], a2a_send.at[n], a2a_recv.at[n], seq=s).start())
+
+    def take(buf, sem, count):
+        v = buf.at[pl.ds(0, count)]
+        pltpu.make_async_copy(v, v, sem).wait()
+
+    def whole(buf, sem):
+        pltpu.make_async_copy(buf, buf, sem).wait()
+
+    stack(kv_cols)
+    to_blocks(put_ref, stack_ref, xkv)
+
+    pl.semaphore_wait(barrier, n_seq - 1 + n_dp - 1)
+    a2a(0, xkv, rkv)
+
+    load_table.wait()
     r = iota((16, 512), 0)
     l = iota((16, 512), 1)
     j = r & 3
@@ -121,51 +168,14 @@
     @pl.when(my_turn)
     def _():
         negs_ref[g * per_ring + lax.div(t, n_dp)] = block.astype(BF)
-
-    def stack(ref, starts):
-        for n, c in enumerate(starts):
-            stack_ref[n * rows:(n + 1) * rows, :] = ref[:, c:c + CH]
-
-    kv_cols = [width + n * CH for n in range(4)] + [3 * width + n * CH for n in range(4)]
-    uq_cols = [n * CH for n in range(4)] + [2 * width + n * CH for n in range(4)]
-    half_cols = [n * CH for n in range(8)]
-
-    def to_blocks(mat, dst):
-        nb = 256 // rb
-        for b in range(slots // 256):
-            y = mm(mat[b * 256:(b + 1) * 256, :], stack_ref[...]).astype(BF)
-            dst[b * nb:(b + 1) * nb] = y.reshape(nb, rb, CH)
-
-    def from_blocks(mat, src, write):
-        v = src[...].reshape(slots, CH)
-        per = 256 // rows
-        for b in range(slots // 256):
-            y = mm(mat[b * 256:(b + 1) * 256, :], v).astype(BF)
-            for n in range(per):
-                write(b * per + n, y[n * rows:(n + 1) * rows])
-
-    def a2a(n, src, dst):
-        dst[t] = src[t]
-        far_first(lambda s: rcopy(src.at[s], dst.at[t], a2a_send.at[n], a2a_recv.at[n], seq=s).start())
-
-    def take(buf, sem, count):
-        v = buf.at[pl.ds(0, count)]
-        pltpu.make_async_copy(v, v, sem).wait()
-
-    stack(qkvu_ref, kv_cols)
-    to_blocks(put_ref, xkv)
-
-    pl.semaphore_wait(barrier, n_seq - 1 + n_dp - 1)
-
-    @pl.when(my_turn)
-    def _():
         mine = negs_ref.at[g * per_ring + lax.div(t, n_dp)]
         far_first(lambda s: rcopy(mine, mine, neg_send, neg_zrecv.at[lax.div(t, n_dp)], seq=s).start())
 
-    a2a(0, xkv, rkv)
-    stack(qkvu_ref, uq_cols)
-    to_blocks(put_ref, xuq)
-    a2a(1, xuq, ruq)
+    for n in range(8):
+        pair_ref[n * rows:(n + 1) * rows, :head] = qkvu_ref[:, 2 * width + n * head:2 * width + (n + 1) * head]
+        pair_ref[n * rows:(n + 1) * rows, head:] = qkvu_ref[:, n * head:(n + 1) * head]
+    to_blocks(put_ref, pair_ref, xq, xu)
+    a2a(1, xq, rq)
 
     i0 = iota((rows, rows), 0)
     l0 = iota((rows, rows), 1)
@@ -198,11 +208,34 @@
     live_col = jnp.where(iota(coef_ref.shape, 0) < own_len, 1.0, 0.0)
     live_ref[...] = (coef_ref[...].astype(F32) * live_col).astype(BF)
 
+    take(rkv, a2a_recv.at[0], n_seq - 1)
+
+    def write_kv(n, y):
+        kv_ref[0, :, n * CH:(n + 1) * CH] = y
+    from_blocks(get_ref, rkv[...], write_kv)
+    odd = lax.rem(t, 2) == 1
+    even = lax.rem(t, 2) == 0
+    mate = t + 1 - 2 * lax.rem(t, 2)
+
+    @pl.when(t + 2 < n_seq)
+    def _():
+        rcopy(kv_ref.at[0], kv_ref.at[2], halo_send.at[1], halo_recv.at[1], seq=lax.rem(t + 2, n_seq)).start()
+
+    @pl.when(even)
+    def _():
+        rcopy(kv_ref.at[0], kv_ref.at[1], halo_send.at[0], halo_recv.at[0], seq=mate).start()
+
+    for lag in range(1, SPAN):
+        @pl.when(t < lag)
+        def _():
+            kv_ref[lag] = jnp.zeros(kv_ref.shape[1:], BF)
+
+    a2a(2, xu, ru)
+
     for k in range(per_ring):
         @pl.when(k * n_dp + g != t)
         def _():
-            v = negs_ref.at[g * per_ring + k]
-            pltpu.make_async_copy(v, v, neg_zrecv.at[k]).wait()
+            whole(negs_ref.at[g * per_ring + k], neg_zrecv.at[k])
     shards = negs_ref.at[pl.ds(g * per_ring, per_ring)]
     each_dp_peer(lambda d: rcopy(shards, shards, neg_xsend, neg_xrecv, dp=d).start())
     take(negs_ref, neg_xrecv, (n_dp - 1) * per_ring)
@@ -217,39 +250,34 @@
     for q in range(4):
         neg_ref[:, q * CH:(q + 1) * CH] = mm(one(l == place + 4 * q), flat).astype(BF)
 
+    load_w.wait()
     head_grad = mm(live_ref[...], neg_ref[...]).astype(BF)
     for b in range(width // CH):
         dmix_ref[:, b * CH:(b + 1) * CH] = mm_nt(head_grad, w_ref[b * CH:(b + 1) * CH, :])
 
-    take(rkv, a2a_recv.at[0], n_seq - 1)
-
-    def write_kv(n, y):
-        kv_ref[0, :, n * CH:(n + 1) * CH] = y
-    from_blocks(get_ref, rkv, write_kv)
-    for lag in range(1, SPAN):
-        @pl.when(t + lag < n_seq)
-        def _():
-            rcopy(kv_ref.at[0], kv_ref.at[lag], halo_send.at[lag - 1], halo_recv.at[lag - 1], seq=lax.rem(t + lag, n_seq)).start()
-
-        @pl.when(t < lag)
-        def _():
-            kv_ref[lag] = jnp.zeros(kv_ref.shape[1:], BF)
-
-    take(ruq, a2a_recv.at[1], n_seq - 1)
-
-    def write_uq(n, y):
-        uq_ref[:, n * CH:(n + 1) * CH] = y
-    from_blocks(get_ref, ruq, write_uq)
-    for lag in range(1, SPAN):
-        @pl.when(t >= lag)
-        def _():
-            pltpu.make_async_copy(kv_ref.at[lag], kv_ref.at[lag], halo_recv.at[lag - 1]).wait()
+    take(rq, a2a_recv.at[1], n_seq - 1)
+
+    def write_q(n, y):
+        q_ref[:, n * head:(n + 1) * head] = y
+    from_blocks(get_ref, rq[...], write_q)
+
+    @pl.when(t >= 2)
+    def _():
+        whole(kv_ref.at[2], halo_recv.at[1])
+
+    @pl.when(odd & (t >= 2))
+    def _():
+        rcopy(kv_ref.at[2], kv_ref.at[1], halo_send.at[0], halo_recv.at[0], seq=mate).start()
+
+    @pl.when(t >= 1)
+    def _():
+        whole(kv_ref.at[1], halo_recv.at[0])
 
     def lanes(h, base=0):
         return pl.ds(pl.multiple_of(base + h * head, head), head)
 
     def forward(h, c):
-        q = uq_ref[:, lanes(h, width)]
+        q = q_ref[:, lanes(h)]
         k3 = kv_ref[:, :, lanes(h, width)].reshape(SPAN * rows, head)
         v3 = kv_ref[:, :, lanes(h)].reshape(SPAN * rows, head)
         s = mm_nt(q, k3) * scale
@@ -264,27 +292,42 @@
     lax.fori_loop(0, HEADS, forward, 0)
 
     step = 32
-    for b in range(rows // step):
-        at = slice(b * step, (b + 1) * step)
+    spans = [slice(b * step, (b + 1) * step) for b in range(rows // step)]
+    for at in spans:
         a = att_ref[at, :]
         cen = a - jnp.mean(a, axis=1, keepdims=True)
         inv = lax.rsqrt(jnp.mean(cen * cen, axis=1, keepdims=True) + eps)
         normed = cen * inv
-        u = uq_ref[at, :width].astype(F32)
+        att_ref[at, :] = normed
+        inv_ref[at, :] = jnp.broadcast_to(inv, (step, 128))
+        du = (dmix_ref[at, :] * normed).astype(BF)
+        for n in range(8):
+            thin_ref[n * rows + at.start:n * rows + at.stop, :] = du[:, n * head:(n + 1) * head]
+    to_blocks(put_back_ref, thin_ref, gu)
+    a2a(3, gu, hu)
+
+    take(ru, a2a_recv.at[2], n_seq - 1)
+
+    def write_u(n, y):
+        u_ref[:, n * head:(n + 1) * head] = y
+    from_blocks(get_ref, ru[...], write_u)
+
+    for at in spans:
+        normed = att_ref[at, :]
+        inv = inv_ref[at, :1]
+        u = u_ref[at, :].astype(F32)
         mixed_ref[at, :] = (normed * u).astype(BF)
-        dm = dmix_ref[at, :]
-        duq_ref[at, :width] = (dm * normed).astype(BF)
-        dn = dm * u
+        dn = dmix_ref[at, :] * u
         da = (dn - jnp.mean(dn, axis=1, keepdims=True) - normed * jnp.mean(dn * normed, axis=1, keepdims=True)) * inv
         datt_ref[at, :] = da.astype(BF)
 
     def backward(h, c):
-        q = uq_ref[:, lanes(h, width)]
+        q = q_ref[:, lanes(h)]
         k3 = kv_ref[:, :, lanes(h, width)].reshape(SPAN * rows, head)
         v3 = kv_ref[:, :, lanes(h)].reshape(SPAN * rows, head)
         da = datt_ref[:, lanes(h)]
         ds = (mm_nt(da, v3) * fac_ref[h]).astype(BF)
-        duq_ref[:, lanes(h, width)] = mm(ds, k3).astype(BF)
+        thin_ref[pl.ds(pl.multiple_of(h * rows, rows), rows), :] = mm(ds, k3).astype(BF)
         kp = mm_tn(ds, q)
         vp = mm_tn(wgt_ref[h], da)
         own_ref[:, lanes(h, width)] = kp[:rows]
@@ -296,18 +339,19 @@
 
     lax.fori_loop(0, HEADS, backward, 0)
 
-    for lag in range(1, SPAN):
-        @pl.when(t >= lag)
-        def _():
-            rcopy(part_ref.at[lag - 1], back_ref.at[lag - 1], back_send.at[lag - 1], back_recv.at[lag - 1], seq=lax.rem(t + n_seq - lag, n_seq)).start()
-
-        @pl.when(t + lag >= n_seq)
-        def _():
-            back_ref[lag - 1] = jnp.zeros(back_ref.shape[1:], BF)
-
-    stack(duq_ref, half_cols)
-    to_blocks(put_back_ref, guq)
-    a2a(2, guq, huq)
+    swap = rcopy(part_ref.at[0], back_ref.at[0], back_send.at[0], back_recv.at[0], seq=mate)
+    swap.start()
+
+    def hand_back():
+        rcopy(part_ref.at[1], back_ref.at[1], back_send.at[1], back_recv.at[1], seq=lax.rem(t + n_seq - 2, n_seq)).start()
+
+    @pl.when(even & (t >= 2))
+    def _():
+        hand_back()
+
+    @pl.when(t + 2 >= n_seq)
+    def _():
+        back_ref[1] = jnp.zeros(back_ref.shape[1:], BF)
 
     per_block = rows // d_rows
     for b in range(width // rows):
@@ -318,8 +362,15 @@
     sum_r[g] = sum_x[g]
     each_dp_peer(lambda d: rcopy(sum_x.at[d], sum_r.at[g], sx_send, sx_recv, dp=d).start())
 
-    for b in range(width // CH):
-        out_ref[:, b * CH:(b + 1) * CH] = mm(mixed_ref[...], w_ref[:, b * CH:(b + 1) * CH]).astype(BF)
+    whole(back_ref.at[0], back_recv.at[0])
+
+    @pl.when(odd & (t >= 2))
+    def _():
+        part_ref[1] = (part_ref[1].astype(F32) + back_ref[0].astype(F32)).astype(BF)
+        hand_back()
+
+    to_blocks(put_back_ref, thin_ref, gq)
+    a2a(4, gq, hq)
 
     take(sum_r, sx_recv, n_dp - 1)
     sum_z[...] = lax.fori_loop(1, n_dp, lambda i, acc: acc + sum_r[i], sum_r[0])
@@ -334,16 +385,19 @@
         def _():
             sum_zr[t] = sum_z[k]
 
-    for lag in range(1, SPAN):
-        @pl.when(t + lag < n_seq)
-        def _():
-            pltpu.make_async_copy(back_ref.at[lag - 1], back_ref.at[lag - 1], back_recv.at[lag - 1]).wait()
+    @pl.when(t + 2 < n_seq)
+    def _():
+        whole(back_ref.at[1], back_recv.at[1])
+    keep = jnp.where(even, 1.0, 0.0)
     for n in range(8):
         c = slice(n * CH, (n + 1) * CH)
-        y = own_ref[:, c] + back_ref[0, :, c].astype(F32) + back_ref[1, :, c].astype(F32)
+        y = own_ref[:, c] + back_ref[0, :, c].astype(F32) * keep + back_ref[1, :, c].astype(F32)
         stack_ref[n * rows:(n + 1) * rows, :] = y.astype(BF)
-    to_blocks(put_back_ref, gkv)
-    a2a(3, gkv, hkv)
+    to_blocks(put_back_ref, stack_ref, gkv)
+    a2a(5, gkv, hkv)
+
+    for b in range(width // CH):
+        out_ref[:, b * CH:(b + 1) * CH] = mm(mixed_ref[...], w_ref[:, b * CH:(b + 1) * CH]).astype(BF)
 
     @pl.when(my_turn)
     def _():
@@ -353,7 +407,7 @@
 
     @pl.when(jnp.logical_not(my_turn))
     def _():
-        pltpu.make_async_copy(sum_f, sum_f, sf_recv).wait()
+        whole(sum_f, sf_recv)
 
     total = sum_f[...]
     top = total.astype(BF)
@@ -371,23 +425,17 @@
             z = jnp.where(lax.rem(g, per) == n, y[:, n * cols:(n + 1) * cols], z)
         dw_ref[...] = z
 
-    take(huq, a2a_recv.at[2], n_seq - 1)
+    take(hu, a2a_recv.at[3], n_seq - 1)
+    take(hq, a2a_recv.at[4], n_seq - 1)
 
     def home_uq(n, y):
-        home_ref[:, uq_cols[n]:uq_cols[n] + CH] = y
-    from_blocks(get_back_ref, huq, home_uq)
-    take(hkv, a2a_recv.at[3], n_seq - 1)
-
-    def home_kv(n, y):
-        home_ref[:, kv_cols[n]:kv_cols[n] + CH] = y
-    from_blocks(get_back_ref, hkv, home_kv)
-
-    for n, buf in enumerate((xkv, xuq, guq, gkv)):
+        home_ref[:, n * head:(n + 1) * head] = y[:, :head]
+        home_ref[:, 2 * width + n * head:2 * width + (n + 1) * head] = y[:, head:]
+    both = jnp.concatenate([hu[...].reshape(slots, head), hq[...].reshape(slots, head)], axis=1)
+    from_blocks(get_back_ref, both, home_uq)
+
+    for n, buf in enumerate((xkv, xq, xu, gu, gq)):
         take(buf, a2a_send.at[n], n_seq - 1)
-
-    def sent(buf, sem):
-        pltpu.make_async_copy(buf, buf, sem).wait()
-
     take(negs_ref, neg_xsend, (n_dp - 1) * per_ring)
     take(sum_x, sx_send, n_dp - 1)
 
@@ -399,15 +447,27 @@
     for k in range(per_ring):
         @pl.when(k * n_dp + g != t)
         def _():
-            sent(sum_z.at[k], sz_send.at[k])
-    for lag in range(1, SPAN):
-        @pl.when(t + lag < n_seq)
-        def _():
-            sent(kv_ref.at[0], halo_send.at[lag - 1])
-
-        @pl.when(t >= lag)
-        def _():
-            sent(part_ref.at[lag - 1], back_send.at[lag - 1])
+            whole(sum_z.at[k], sz_send.at[k])
+
+    @pl.when(t + 2 < n_seq)
+    def _():
+        whole(kv_ref.at[0], halo_send.at[1])
+
+    @pl.when(even | (t >= 2))
+    def _():
+        whole(kv_ref.at[0], halo_send.at[0])
+    whole(part_ref.at[0], back_send.at[0])
+
+    @pl.when(t >= 2)
+    def _():
+        whole(part_ref.at[1], back_send.at[1])
+
+    take(hkv, a2a_recv.at[5], n_seq - 1)
+
+    def home_kv(n, y):
+        home_ref[:, kv_cols[n]:kv_cols[n] + CH] = y
+    from_blocks(get_back_ref, hkv[...], home_kv)
+    take(gkv, a2a_send.at[5], n_seq - 1)
 
 
 def on_device(n_dp, n_seq, qkvu, w_out, head_coef, item_table, neg_ids, send_order, recv_order, tile_len):
@@ -421,30 +481,36 @@
     vm = pl.BlockSpec(memory_space=pltpu.VMEM)
     sm = pl.BlockSpec(memory_space=pltpu.SMEM)
     dma = pltpu.SemaphoreType.DMA
-    blocks = pltpu.VMEM((n_seq, rb, CH), BF)
+    any_space = pl.BlockSpec(memory_space=pl.ANY)
+    wide = pltpu.VMEM((n_seq, rb, CH), BF)
+    thin = pltpu.VMEM((n_seq, rb, CH // 2), BF)
     square = pltpu.VMEM((slots, slots), BF)
     return pl.pallas_call(
         functools.partial(kernel, n_dp, n_seq),
         out_shape=(
-            jax.ShapeDtypeStruct((rows, width), BF),
-            jax.ShapeDtypeStruct((rows, 4 * width), BF),
-            jax.ShapeDtypeStruct((d_rows, width // n_dp), F32),
+            pltpu.VMEM((rows, width), BF),
+            pltpu.VMEM((rows, 4 * width), BF),
+            pltpu.VMEM((d_rows, width // n_dp), F32),
         ),
-        in_specs=[sm, sm] + [vm] * 6,
+        in_specs=[sm, sm, vm, vm, vm, vm, any_space, any_space],
         out_specs=(vm, vm, vm),
         scratch_shapes=[
-            square, square, square, square, pltpu.VMEM((slots, CH), BF),
-            blocks, blocks, blocks, blocks, blocks, blocks, blocks, blocks,
+            pltpu.VMEM(w_out.shape, BF), pltpu.VMEM(item_table.shape, BF),
+            square, square, square, square,
+            pltpu.VMEM((slots, CH), BF), pltpu.VMEM((slots, CH), BF), pltpu.VMEM((slots, CH // 2), BF),
+            wide, wide, wide, wide,
+            thin, thin, thin, thin, thin, thin, thin, thin,
             pltpu.VMEM((SPAN, rows, 2 * width), BF),
-            pltpu.VMEM((rows, 2 * width), BF),
+            pltpu.VMEM((rows, width), BF),
+            pltpu.VMEM((rows, width), BF),
             pltpu.VMEM((rows, 2 * width), F32),
-            pltpu.VMEM((rows, 2 * width), BF),
             pltpu.VMEM((SPAN - 1, rows, 2 * width), BF),
             pltpu.VMEM((SPAN - 1, rows, 2 * width), BF),
             pltpu.VMEM((HEADS, rows, SPAN * rows), BF),
             pltpu.VMEM((HEADS, rows, SPAN * rows), F32),
             pltpu.VMEM((rows, SPAN * rows), F32),
             pltpu.VMEM((rows, width), F32),
+            pltpu.VMEM((rows, 128), F32),
             pltpu.VMEM((rows, width), BF),
             pltpu.VMEM((rows, width), BF),
             pltpu.VMEM((rows, negs), BF),
@@ -456,14 +522,14 @@
             pltpu.VMEM((per_ring, d_rows, negs), F32),
             pltpu.VMEM((n_seq, d_rows, negs), F32),
             pltpu.VMEM((d_rows, negs), F32),
-            dma((4,)), dma((4,)), dma, dma((per_ring,)), dma, dma,
+            dma((2,)), dma((6,)), dma((6,)), dma, dma((per_ring,)), dma, dma,
             dma((SPAN - 1,)), dma((SPAN - 1,)), dma((SPAN - 1,)), dma((SPAN - 1,)),
             dma, dma, dma((per_ring,)), dma, dma, dma,
         ],
         compiler_params=pltpu.CompilerParams(
             collective_id=0, has_side_effects=True, vmem_limit_bytes=60 * 2**20
         ),
-    )(neg_ids, tile_len, qkvu, w_out, head_coef, item_table, send_order, recv_order)
+    )(neg_ids, tile_len, qkvu, head_coef, send_order, recv_order, w_out, item_table)
 
 
 def solution(mesh):

time: 276 us -> 257 us (0.931)
  the two profiles are of different devices: /device:TPU:17 before, /device:TPU:15 now
where the time goes in v2:
time: 257 us; the launch traced here: 256 us
  Pallas kernels  254 us (99%)
    pallas_call x1, Pallas kernels, on_device(): pl.pallas_call(functools.partial(kernel, n_dp, n_seq), out_shape=(pltpu.V...  254 us

profile of v2, /device:TPU:15, one launch (start us, length us, event | category | flops | bytes accessed | tf_op | source)
XLA Modules:
  0.0 256.4 jit_solution(14638581895688998598)
XLA Ops:
  0.6 253.5 %shard_map.103 = (bf16[128,1024]{1,0:T(8,128)(2,1)S(1)}, bf16[128,4096]{1,0:T(8,128)(2,1)S(1)}, f32[16,64]{1,0:T(8,128)S(1)}) custom-call(s32[4]{0:T(128)} %ids_ref.1, s32[1,64]{1,0:T(1,128)} %len_ref.1, bf16[128,4096]{1,0:T(8,128)(2,1)} %qkvu_ref.1, bf16[128,256]{1,0:T(8,128)(2,1)} %coef_ref.1, s32[1,128]{1,0:T(1,128)} %send_ref.1, s32[1,128]{1,0:T(1,128)} %recv_ref.1, ...), custom_call_target="tpu_custom_call" | custom-call | tf_op jit(solution)/shard_map/pallas_call | solution.py:488
  254.2 0.7 copy.14
  254.9 0.6 copy.16
  255.5 1.0 copy.15

commit v3 on v2

--- a/solution.py
+++ b/solution.py
@@ -35,9 +35,9 @@
 
 def kernel(
     n_dp, n_seq,
-    ids_ref, len_ref, qkvu_ref, coef_ref, send_ref, recv_ref, w_hbm, table_hbm,
+    ids_ref, len_ref, qkvu_hbm, coef_hbm, send_hbm, recv_hbm, w_hbm, table_hbm,
     out_ref, home_ref, dw_ref,
-    w_ref, table_ref,
+    send_ref, recv_ref, qkvu_ref, coef_ref, table_ref, w_ref,
     put_ref, get_ref, put_back_ref, get_back_ref, stack_ref, pair_ref, thin_ref,
     xkv, rkv, gkv, hkv,
     xq, xu, rq, ru, gq, gu, hq, hu,
@@ -54,10 +54,13 @@
     slots = 8 * rows
     head = width // HEADS
     scale = 1.0 / math.sqrt(head)
-    per_ring = n_seq // n_dp
+    plane = 2 * n_dp
+    per_ring = n_seq // plane
     d_rows = width // n_seq
     rb = slots // n_seq
-    my_turn = lax.rem(t, n_dp) == g
+    carrier = 2 * g + lax.rem(t, 2)
+    mate = t + 1 - 2 * lax.rem(t, 2)
+    my_turn = lax.rem(lax.div(t, 2), n_dp) == g
 
     def rcopy(src, dst, ssem, rsem, **where):
         return pltpu.make_async_remote_copy(
@@ -90,14 +93,34 @@
             return c
         lax.fori_loop(1, n_dp, step, 0)
 
+    def each_plane_peer(copy):
+        def step(i, c):
+            d = lax.rem(g + i, n_dp)
+
+            @pl.when(i > 0)
+            def _():
+                copy(2 * d + lax.rem(t, 2), {"dp": d}).start()
+            copy(2 * d + 1 - lax.rem(t, 2), {"dp": d, "seq": mate}).start()
+            return c
+        lax.fori_loop(0, n_dp, step, 0)
+
+    loads = [
+        pltpu.make_async_copy(src, dst, load_sem.at[n])
+        for n, (src, dst) in enumerate((
+            (send_hbm, send_ref), (recv_hbm, recv_ref), (qkvu_hbm, qkvu_ref),
+            (coef_hbm, coef_ref), (table_hbm, table_ref), (w_hbm, w_ref),
+        ))
+    ]
+    for load in loads:
+        load.start()
+
     barrier = pltpu.get_barrier_semaphore()
     each_seq_peer(lambda s: pl.semaphore_signal(barrier, inc=1, device_id={"seq": s}, device_id_type=MESH))
     each_dp_peer(lambda d: pl.semaphore_signal(barrier, inc=1, device_id={"dp": d}, device_id_type=MESH))
-
-    load_table = pltpu.make_async_copy(table_hbm, table_ref, load_sem.at[0])
-    load_w = pltpu.make_async_copy(w_hbm, w_ref, load_sem.at[1])
-    load_table.start()
-    load_w.start()
+    each_dp_peer(lambda d: pl.semaphore_signal(barrier, inc=1, device_id={"dp": d, "seq": mate}, device_id_type=MESH))
+
+    loads[0].wait()
+    loads[1].wait()
 
     send_f = send_ref[...].astype(F32)
     recv_f = recv_ref[...].astype(F32)
@@ -149,13 +172,14 @@
     def whole(buf, sem):
         pltpu.make_async_copy(buf, buf, sem).wait()
 
+    loads[2].wait()
     stack(kv_cols)
     to_blocks(put_ref, stack_ref, xkv)
 
-    pl.semaphore_wait(barrier, n_seq - 1 + n_dp - 1)
+    pl.semaphore_wait(barrier, n_seq - 1 + 2 * (n_dp - 1))
     a2a(0, xkv, rkv)
 
-    load_table.wait()
+    loads[4].wait()
     r = iota((16, 512), 0)
     l = iota((16, 512), 1)
     j = r & 3
@@ -167,9 +191,15 @@
 
     @pl.when(my_turn)
     def _():
-        negs_ref[g * per_ring + lax.div(t, n_dp)] = block.astype(BF)
-        mine = negs_ref.at[g * per_ring + lax.div(t, n_dp)]
-        far_first(lambda s: rcopy(mine, mine, neg_send, neg_zrecv.at[lax.div(t, n_dp)], seq=s).start())
+        k = lax.div(t, plane)
+        negs_ref[carrier * per_ring + k] = block.astype(BF)
+        mine = negs_ref.at[carrier * per_ring + k]
+
+        def step(i, c):
+            s = lax.rem(t + 2 * i, n_seq)
+            rcopy(mine, mine, neg_send, neg_zrecv.at[k], seq=s).start()
+            return c
+        lax.fori_loop(1, n_seq // 2, step, 0)
 
     for n in range(8):
         pair_ref[n * rows:(n + 1) * rows, :head] = qkvu_ref[:, 2 * width + n * head:2 * width + (n + 1) * head]
@@ -205,6 +235,7 @@
     for n, m in enumerate((alive & (l0 <= i0) & (l0 < own_len), alive & (l0 < len_1), alive & (l0 < len_2))):
         mask_ref[:, n * rows:(n + 1) * rows] = jnp.where(m, 1.0 / rows, 0.0)
 
+    loads[3].wait()
     live_col = jnp.where(iota(coef_ref.shape, 0) < own_len, 1.0, 0.0)
     live_ref[...] = (coef_ref[...].astype(F32) * live_col).astype(BF)
 
@@ -215,7 +246,6 @@
     from_blocks(get_ref, rkv[...], write_kv)
     odd = lax.rem(t, 2) == 1
     even = lax.rem(t, 2) == 0
-    mate = t + 1 - 2 * lax.rem(t, 2)
 
     @pl.when(t + 2 < n_seq)
     def _():
@@ -233,24 +263,24 @@
     a2a(2, xu, ru)
 
     for k in range(per_ring):
-        @pl.when(k * n_dp + g != t)
+        @pl.when(k * plane + carrier != t)
         def _():
-            whole(negs_ref.at[g * per_ring + k], neg_zrecv.at[k])
-    shards = negs_ref.at[pl.ds(g * per_ring, per_ring)]
-    each_dp_peer(lambda d: rcopy(shards, shards, neg_xsend, neg_xrecv, dp=d).start())
-    take(negs_ref, neg_xrecv, (n_dp - 1) * per_ring)
+            whole(negs_ref.at[carrier * per_ring + k], neg_zrecv.at[k])
+    shards = negs_ref.at[pl.ds(carrier * per_ring, per_ring)]
+    each_plane_peer(lambda c, where: rcopy(shards, shards, neg_xsend, neg_xrecv, **where))
+    take(negs_ref, neg_xrecv, (plane - 1) * per_ring)
 
     n_negs = 4 * n_seq
     flat = negs_ref[...].reshape(16 * n_seq, CH)
     n = iota((n_negs, 16 * n_seq), 0)
     l = iota((n_negs, 16 * n_seq), 1)
     shard = lax.shift_right_logical(n, 2)
-    ring_bits = n_dp.bit_length() - 1
-    place = ((shard & (n_dp - 1)) * per_ring + lax.shift_right_logical(shard, ring_bits)) * 16 + (n & 3)
+    ring_bits = plane.bit_length() - 1
+    place = ((shard & (plane - 1)) * per_ring + lax.shift_right_logical(shard, ring_bits)) * 16 + (n & 3)
     for q in range(4):
         neg_ref[:, q * CH:(q + 1) * CH] = mm(one(l == place + 4 * q), flat).astype(BF)
 
-    load_w.wait()
+    loads[5].wait()
     head_grad = mm(live_ref[...], neg_ref[...]).astype(BF)
     for b in range(width // CH):
         dmix_ref[:, b * CH:(b + 1) * CH] = mm_nt(head_grad, w_ref[b * CH:(b + 1) * CH, :])
@@ -358,9 +388,10 @@
         y = mm_tn(mixed_ref[:, b * rows:(b + 1) * rows], live_ref[...])
         for n in range(per_block):
             s = b * per_block + n
-            sum_x[s % n_dp, s // n_dp] = y[n * d_rows:(n + 1) * d_rows]
-    sum_r[g] = sum_x[g]
-    each_dp_peer(lambda d: rcopy(sum_x.at[d], sum_r.at[g], sx_send, sx_recv, dp=d).start())
+            sum_x[s % plane * per_ring + s // plane] = y[n * d_rows:(n + 1) * d_rows]
+    own_at = pl.ds(carrier * per_ring, per_ring)
+    sum_r[own_at] = sum_x[own_at]
+    each_plane_peer(lambda c, where: rcopy(sum_x.at[pl.ds(c * per_ring, per_ring)], sum_r.at[own_at], sx_send, sx_recv, **where))
 
     whole(back_ref.at[0], back_recv.at[0])
 
@@ -372,18 +403,19 @@
     to_blocks(put_back_ref, thin_ref, gq)
     a2a(4, gq, hq)
 
-    take(sum_r, sx_recv, n_dp - 1)
-    sum_z[...] = lax.fori_loop(1, n_dp, lambda i, acc: acc + sum_r[i], sum_r[0])
+    take(sum_r, sx_recv, (plane - 1) * per_ring)
+    chip = lax.div(t, 2)
     for k in range(per_ring):
-        s = k * n_dp + g
+        s = k * plane + carrier
+        sum_z[k] = lax.fori_loop(1, plane, lambda i, acc: acc + sum_r[i * per_ring + k], sum_r[k]).astype(BF)
 
         @pl.when(s != t)
         def _():
-            rcopy(sum_z.at[k], sum_zr.at[t], sz_send.at[k], sz_recv, seq=s).start()
+            rcopy(sum_z.at[k], sum_zr.at[chip], sz_send.at[k], sz_recv, seq=s).start()
 
         @pl.when(s == t)
         def _():
-            sum_zr[t] = sum_z[k]
+            sum_zr[chip] = sum_z[k]
 
     @pl.when(t + 2 < n_seq)
     def _():
@@ -401,8 +433,8 @@
 
     @pl.when(my_turn)
     def _():
-        take(sum_zr, sz_recv, n_seq - 1)
-        sum_f[...] = lax.fori_loop(1, n_seq, lambda i, acc: acc + sum_zr[i], sum_zr[0])
+        take(sum_zr, sz_recv, n_seq // 2 - 1)
+        sum_f[...] = lax.fori_loop(1, n_seq // 2, lambda i, acc: acc + sum_zr[i].astype(F32), sum_zr[0].astype(F32))
         each_dp_peer(lambda d: rcopy(sum_f, sum_f, sf_send, sf_recv, dp=d).start())
 
     @pl.when(jnp.logical_not(my_turn))
@@ -436,16 +468,16 @@
 
     for n, buf in enumerate((xkv, xq, xu, gu, gq)):
         take(buf, a2a_send.at[n], n_seq - 1)
-    take(negs_ref, neg_xsend, (n_dp - 1) * per_ring)
-    take(sum_x, sx_send, n_dp - 1)
+    take(negs_ref, neg_xsend, (plane - 1) * per_ring)
+    take(sum_x, sx_send, (plane - 1) * per_ring)
 
     @pl.when(my_turn)
     def _():
-        take(negs_ref, neg_send, n_seq - 1)
-        take(sum_zr, sf_send, n_dp - 1)
+        take(negs_ref, neg_send, n_seq // 2 - 1)
+        take(sum_r, sf_send, n_dp - 1)
 
     for k in range(per_ring):
-        @pl.when(k * n_dp + g != t)
+        @pl.when(k * plane + carrier != t)
         def _():
             whole(sum_z.at[k], sz_send.at[k])
 
@@ -468,6 +500,14 @@
         home_ref[:, kv_cols[n]:kv_cols[n] + CH] = y
     from_blocks(get_back_ref, hkv[...], home_kv)
     take(gkv, a2a_send.at[5], n_seq - 1)
+
+
+def put_out(a, b, c, out_a, out_b, out_c, sem):
+    copies = [pltpu.make_async_copy(x, y, sem.at[n]) for n, (x, y) in enumerate(((a, out_a), (b, out_b), (c, out_c)))]
+    for copy in copies:
+        copy.start()
+    for copy in copies:
+        copy.wait()
 
 
 def on_device(n_dp, n_seq, qkvu, w_out, head_coef, item_table, neg_ids, send_order, recv_order, tile_len):
@@ -475,7 +515,7 @@
     width = w_out.shape[0]
     slots = 8 * rows
     rb = slots // n_seq
-    per_ring = n_seq // n_dp
+    per_ring = n_seq // (2 * n_dp)
     d_rows = width // n_seq
     negs = head_coef.shape[1]
     vm = pl.BlockSpec(memory_space=pltpu.VMEM)
@@ -485,17 +525,19 @@
     wide = pltpu.VMEM((n_seq, rb, CH), BF)
     thin = pltpu.VMEM((n_seq, rb, CH // 2), BF)
     square = pltpu.VMEM((slots, slots), BF)
-    return pl.pallas_call(
+    results = pl.pallas_call(
         functools.partial(kernel, n_dp, n_seq),
         out_shape=(
             pltpu.VMEM((rows, width), BF),
             pltpu.VMEM((rows, 4 * width), BF),
             pltpu.VMEM((d_rows, width // n_dp), F32),
         ),
-        in_specs=[sm, sm, vm, vm, vm, vm, any_space, any_space],
+        in_specs=[sm, sm] + [any_space] * 6,
         out_specs=(vm, vm, vm),
         scratch_shapes=[
-            pltpu.VMEM(w_out.shape, BF), pltpu.VMEM(item_table.shape, BF),
+            pltpu.VMEM(send_order.shape, jnp.int32), pltpu.VMEM(recv_order.shape, jnp.int32),
+            pltpu.VMEM(qkvu.shape, BF), pltpu.VMEM(head_coef.shape, BF),
+            pltpu.VMEM(item_table.shape, BF), pltpu.VMEM(w_out.shape, BF),
             square, square, square, square,
             pltpu.VMEM((slots, CH), BF), pltpu.VMEM((slots, CH), BF), pltpu.VMEM((slots, CH // 2), BF),
             wide, wide, wide, wide,
@@ -517,12 +559,12 @@
             pltpu.VMEM((rows, width), F32),
             pltpu.VMEM((n_seq, 16, CH), BF),
             pltpu.VMEM((negs, width), BF),
-            pltpu.VMEM((n_dp, per_ring, d_rows, negs), F32),
-            pltpu.VMEM((n_dp, per_ring, d_rows, negs), F32),
-            pltpu.VMEM((per_ring, d_rows, negs), F32),
             pltpu.VMEM((n_seq, d_rows, negs), F32),
+            pltpu.VMEM((n_seq, d_rows, negs), F32),
+            pltpu.VMEM((per_ring, d_rows, negs), BF),
+            pltpu.VMEM((n_seq // 2, d_rows, negs), BF),
             pltpu.VMEM((d_rows, negs), F32),
-            dma((2,)), dma((6,)), dma((6,)), dma, dma((per_ring,)), dma, dma,
+            dma((6,)), dma((6,)), dma((6,)), dma, dma((per_ring,)), dma, dma,
             dma((SPAN - 1,)), dma((SPAN - 1,)), dma((SPAN - 1,)), dma((SPAN - 1,)),
             dma, dma, dma((per_ring,)), dma, dma, dma,
         ],
@@ -530,6 +572,14 @@
             collective_id=0, has_side_effects=True, vmem_limit_bytes=60 * 2**20
         ),
     )(neg_ids, tile_len, qkvu, head_coef, send_order, recv_order, w_out, item_table)
+    return pl.pallas_call(
+        put_out,
+        out_shape=tuple(jax.ShapeDtypeStruct(r.shape, r.dtype) for r in results),
+        in_specs=[pl.BlockSpec(memory_space=pltpu.VMEM)] * 3,
+        out_specs=(any_space,) * 3,
+        scratch_shapes=[dma((3,))],
+        compiler_params=pltpu.CompilerParams(vmem_limit_bytes=4 * 2**20),
+    )(*results)
 
 
 def solution(mesh):

time: 257 us -> 264 us (1.027)
  the two profiles are of different devices: /device:TPU:15 before, /device:TPU:31 now
where the time goes in v3:
time: 264 us
  Pallas kernels  263 us (100%)
    pallas_call x1, Pallas kernels, on_device(): pl.pallas_call(functools.partial(kernel, n_dp, n_seq), out_shape=(pltpu.V...  262 us

profile of v3, /device:TPU:31, one launch (start us, length us, event | category | flops | bytes accessed | tf_op | source)
XLA Modules:
  0.0 263.8 jit_solution(4909993831838584606)
XLA Ops:
  0.6 262.1 %shard_map.103 = (bf16[128,1024]{1,0:T(8,128)(2,1)S(1)}, bf16[128,4096]{1,0:T(8,128)(2,1)S(1)}, f32[16,64]{1,0:T(8,128)S(1)}) custom-call(s32[4]{0:T(128)} %ids_ref.1, s32[1,64]{1,0:T(1,128)} %len_ref.1, bf16[128,4096]{1,0:T(8,128)(2,1)} %qkvu_hbm.1, bf16[128,256]{1,0:T(8,128)(2,1)} %coef_hbm.1, s32[1,128]{1,0:T(1,128)} %send_hbm.1, s32[1,128]{1,0:T(1,128)} %recv_hbm.1, ...), custom_call_target="tpu_custom_call" | custom-call | tf_op jit(solution)/shard_map/pallas_call | solution.py:528
  262.7 1.1 shard_map.104

commit v4 on v2

--- a/solution.py
+++ b/solution.py
@@ -373,7 +373,7 @@
     a2a(4, gq, hq)
 
     take(sum_r, sx_recv, n_dp - 1)
-    sum_z[...] = lax.fori_loop(1, n_dp, lambda i, acc: acc + sum_r[i], sum_r[0])
+    sum_z[...] = lax.fori_loop(1, n_dp, lambda i, acc: acc + sum_r[i], sum_r[0]).astype(BF)
     for k in range(per_ring):
         s = k * n_dp + g
 
@@ -402,8 +402,8 @@
     @pl.when(my_turn)
     def _():
         take(sum_zr, sz_recv, n_seq - 1)
-        sum_f[...] = lax.fori_loop(1, n_seq, lambda i, acc: acc + sum_zr[i], sum_zr[0])
-        each_dp_peer(lambda d: rcopy(sum_f, sum_f, sf_send, sf_recv, dp=d).start())
+        sum_f[...] = lax.fori_loop(1, n_seq, lambda i, acc: acc + sum_zr[i].astype(F32), sum_zr[0].astype(F32))
+        each_dp_peer(lambda d: rcopy(sum_f, sum_f, sf_send.at[d], sf_recv, dp=d).start())
 
     @pl.when(jnp.logical_not(my_turn))
     def _():
@@ -442,7 +442,7 @@
     @pl.when(my_turn)
     def _():
         take(negs_ref, neg_send, n_seq - 1)
-        take(sum_zr, sf_send, n_dp - 1)
+        each_dp_peer(lambda d: whole(sum_f, sf_send.at[d]))
 
     for k in range(per_ring):
         @pl.when(k * n_dp + g != t)
@@ -468,6 +468,14 @@
         home_ref[:, kv_cols[n]:kv_cols[n] + CH] = y
     from_blocks(get_back_ref, hkv[...], home_kv)
     take(gkv, a2a_send.at[5], n_seq - 1)
+
+
+def put_out(a, b, c, out_a, out_b, out_c, sem):
+    copies = [pltpu.make_async_copy(x, y, sem.at[n]) for n, (x, y) in enumerate(((a, out_a), (b, out_b), (c, out_c)))]
+    for copy in copies:
+        copy.start()
+    for copy in copies:
+        copy.wait()
 
 
 def on_device(n_dp, n_seq, qkvu, w_out, head_coef, item_table, neg_ids, send_order, recv_order, tile_len):
@@ -485,7 +493,7 @@
     wide = pltpu.VMEM((n_seq, rb, CH), BF)
     thin = pltpu.VMEM((n_seq, rb, CH // 2), BF)
     square = pltpu.VMEM((slots, slots), BF)
-    return pl.pallas_call(
+    results = pl.pallas_call(
         functools.partial(kernel, n_dp, n_seq),
         out_shape=(
             pltpu.VMEM((rows, width), BF),
@@ -519,17 +527,25 @@
             pltpu.VMEM((negs, width), BF),
             pltpu.VMEM((n_dp, per_ring, d_rows, negs), F32),
             pltpu.VMEM((n_dp, per_ring, d_rows, negs), F32),
-            pltpu.VMEM((per_ring, d_rows, negs), F32),
-            pltpu.VMEM((n_seq, d_rows, negs), F32),
+            pltpu.VMEM((per_ring, d_rows, negs), BF),
+            pltpu.VMEM((n_seq, d_rows, negs), BF),
             pltpu.VMEM((d_rows, negs), F32),
             dma((2,)), dma((6,)), dma((6,)), dma, dma((per_ring,)), dma, dma,
             dma((SPAN - 1,)), dma((SPAN - 1,)), dma((SPAN - 1,)), dma((SPAN - 1,)),
-            dma, dma, dma((per_ring,)), dma, dma, dma,
+            dma, dma, dma((per_ring,)), dma, dma((n_dp,)), dma,
         ],
         compiler_params=pltpu.CompilerParams(
             collective_id=0, has_side_effects=True, vmem_limit_bytes=60 * 2**20
         ),
     )(neg_ids, tile_len, qkvu, head_coef, send_order, recv_order, w_out, item_table)
+    return pl.pallas_call(
+        put_out,
+        out_shape=tuple(jax.ShapeDtypeStruct(r.shape, r.dtype) for r in results),
+        in_specs=[vm] * 3,
+        out_specs=(any_space,) * 3,
+        scratch_shapes=[dma((3,))],
+        compiler_params=pltpu.CompilerParams(vmem_limit_bytes=4 * 2**20),
+    )(*results)
 
 
 def solution(mesh):

time: 257 us -> 251 us (0.977)
  Pallas kernels: 254 us -> 250 us
    pallas_call x1, Pallas kernels: 254 us -> 249 us  [on_device(): pl.pallas_call(functools.partial(kernel, n_dp, n_seq), out_shape=(pltpu.V...]
where the time goes in v4:
time: 251 us
  Pallas kernels  250 us (100%)
    pallas_call x1, Pallas kernels, on_device(): pl.pallas_call(functools.partial(kernel, n_dp, n_seq), out_shape=(pltpu.V...  249 us

profile of v4, /device:TPU:15, one launch (start us, length us, event | category | flops | bytes accessed | tf_op | source)
XLA Modules:
  0.0 251.1 jit_solution(17420835629352008770)
XLA Ops:
  0.6 249.4 %shard_map.103 = (bf16[128,1024]{1,0:T(8,128)(2,1)S(1)}, bf16[128,4096]{1,0:T(8,128)(2,1)S(1)}, f32[16,64]{1,0:T(8,128)S(1)}) custom-call(s32[4]{0:T(128)} %ids_ref.1, s32[1,64]{1,0:T(1,128)} %len_ref.1, bf16[128,4096]{1,0:T(8,128)(2,1)} %qkvu_ref.1, bf16[128,256]{1,0:T(8,128)(2,1)} %coef_ref.1, s32[1,128]{1,0:T(1,128)} %send_ref.1, s32[1,128]{1,0:T(1,128)} %recv_ref.1, ...), custom_call_target="tpu_custom_call" | custom-call | tf_op jit(solution)/shard_map/pallas_call | solution.py:496
  250.0 1.1 shard_map.104
